TPU v7x, 512 devices: a whole 4x8x8 slice. The times are simulated.
512 devices in a mesh: dp: 32 (over x, y), seq: 16 (over z, core).
Axes of the slice: x: 4, y: 8, z: 8, core: 2. Of those that a mesh axis runs over, the one named last changes fastest.
Arguments:
- residual_stream: bfloat16 [262144, 2048], P(('dp', 'seq')), parts along dimension 0, may hold values from -6 to 6
- octet_readout: bfloat16 [256, 2048], replicated, may hold values from -6 to 6
- downsampling_filter: bfloat16 [32, 256, 96], replicated, may hold values from -0.375 to 0.375
- sharpness_factor: float32 [8], replicated, may hold values from 4 to 20
- widening_filter: bfloat16 [32, 32, 256], replicated, may hold values from -2 to 2
Outputs:
- logits: bfloat16 [262144, 256], P(('dp', 'seq')), parts along dimension 0
There are 32 independent parts, one for each index of `dp`. A program takes and returns all parts, laid end to end along the dimension named above; an argument that names none is the same for every part. Nothing has to cross between parts.
All inputs are finite; a program needn't handle non-finite values.
Results may differ from a plain program's by a relative error of at most 0.0052.
Values may be sent and summed in bfloat16 or wider, within the bound.
A program may use at most 64 MiB of HBM per device.

v0:
```python
import jax
import jax.numpy as jnp
from jax import lax
from jax.sharding import PartitionSpec as P

SHORTEN = 4


def shifted_2(array, axis, by):
    count = lax.axis_size(axis)
    pairs = [(i, i + by) for i in range(count) if 0 <= i + by < count]
    return lax.ppermute(array, axis, pairs)


def passed_along(block, axis, distance):
    devices = range(lax.axis_size(axis))
    route = [((i - distance) % len(devices), i) for i in devices]
    return lax.ppermute(block, axis, route)


def normalize(vectors):
    return vectors * lax.rsqrt(jnp.sum(vectors * vectors, axis=-1, keepdims=True) + 1e-06)


def shorten(shifted, kernel_part, groups):
    byte_rows, model_width = shifted.shape
    windows = shifted.reshape(byte_rows // SHORTEN, SHORTEN, groups, model_width // groups)
    kernel = kernel_part.reshape(groups, SHORTEN, model_width // groups, kernel_part.shape[2])
    return jnp.einsum("jtgc,gtco->jgo", windows, kernel, preferred_element_type=jnp.float32)


def on_device(
    residual_stream, octet_readout, downsampling_filter, sharpness_factor, widening_filter
):
    byte_rows = residual_stream.shape[0]
    model_width = residual_stream.shape[1]
    groups = downsampling_filter.shape[0]
    group_width = model_width // groups
    per_group = downsampling_filter.shape[2] // 3
    attention_number = sharpness_factor.shape[0]
    head_size = groups * per_group // attention_number
    tokens_here = byte_rows // SHORTEN
    rim_rows = SHORTEN - 1
    left_rim = shifted_2(residual_stream[byte_rows - rim_rows :], "seq", 1)
    shifted = jnp.concatenate([left_rim, residual_stream[: byte_rows - rim_rows]], 0)
    mixed_out = shorten(shifted, downsampling_filter, groups)
    queries = normalize(
        mixed_out[:, :, :per_group].reshape(tokens_here, attention_number, head_size)
    ).astype(jnp.bfloat16)
    key_unit = normalize(
        mixed_out[:, :, per_group : 2 * per_group].reshape(tokens_here, attention_number, head_size)
    ).astype(jnp.bfloat16)
    values = (
        mixed_out[:, :, 2 * per_group :]
        .reshape(tokens_here, attention_number, head_size)
        .astype(jnp.bfloat16)
    )
    my_index = lax.axis_index("seq")
    first_token = my_index * tokens_here
    sharpness_vertical = sharpness_factor[:, None, None]
    query_pos = first_token + jnp.arange(tokens_here, dtype=jnp.int32)
    stacked = jnp.stack([key_unit, values], 0)
    gathered = lax.all_gather(stacked, "seq", axis=1, tiled=True)
    all_keys, all_values = (gathered[0], gathered[1])
    similarity_matrix = (
        jnp.einsum("jsg,isg->sji", queries, all_keys, preferred_element_type=jnp.float32)
        * sharpness_vertical
    )
    key_pos = jnp.arange(all_keys.shape[0], dtype=jnp.int32)
    future_masked = key_pos[None, :] <= query_pos[:, None]
    softmax_shares = jnp.where(
        future_masked[None],
        jnp.exp(similarity_matrix - sharpness_vertical),
        jnp.zeros((), jnp.float32),
    )
    denom_sum = jnp.sum(softmax_shares, axis=-1)
    weighted = jnp.einsum(
        "hqk,khd->qhd",
        softmax_shares.astype(jnp.bfloat16),
        all_values,
        preferred_element_type=jnp.float32,
    )
    attended = (weighted / jnp.transpose(denom_sum)[:, :, None]).astype(jnp.bfloat16)
    attended = attended.reshape(tokens_here, groups, per_group)
    upsampled = jnp.einsum(
        "jgc,gcu->jgu", attended, widening_filter, preferred_element_type=jnp.float32
    )
    upsampled = (
        upsampled.reshape(tokens_here, groups, SHORTEN, group_width)
        .transpose(0, 2, 1, 3)
        .reshape(byte_rows, model_width)
    )
    hidden = residual_stream.astype(jnp.float32) + upsampled
    normed = (hidden * lax.rsqrt(jnp.mean(hidden * hidden, axis=-1, keepdims=True) + 1e-05)).astype(
        jnp.bfloat16
    )
    logits = lax.dot_general(
        normed, octet_readout, (((1,), (1,)), ((), ())), preferred_element_type=jnp.float32
    ) * model_width ** (-0.5)
    return logits.astype(jnp.bfloat16)


def solution(mesh):
    in_specs = (P(("dp", "seq"), None), P(), P(), P(), P())
    out_specs = P(("dp", "seq"), None)
    return jax.shard_map(
        on_device, mesh=mesh, in_specs=in_specs, out_specs=out_specs, check_vma=False
    )
```

profile of v0, /device:TPU:1, one launch (start us, length us, event | category | flops | bytes accessed | tf_op | source)
XLA Modules:
  0.0 155.1 jit_solution(6165816291397608881)
XLA Ops:
  6.5 0.0 copy-start
  6.5 0.0 copy-start.2
  6.5 0.0 all-gather.2.cloned.1.call-start
  6.5 0.9 slice.22
  7.5 5.5 %collective-permute-start = (bf16[3,2048]{1,0:T(4,128)(2,1)S(1)}, bf16[3,2048]{1,0:T(4,128)(2,1)S(1)}, u32[]{:S(2)}, u32[]{:S(2)}) collective-permute-start(bf16[3,2048]{1,0:T(4,128)(2,1)S(1)} %slice.22), channel_id=1, source_target_pairs={{0,1},{1,2},{2,3},{3,4},{4,5},{5,6},{6,7},{7,8},{8,9},{9,10},{10,1... | collective-permute-start | bytes 36872 | tf_op jit(solution)/shard_map/ppermute | solution.py:12
  13.0 3.9 %copy.12 = bf16[32,256,96]{2,1,0:T(8,128)(2,1)} copy(bf16[32,256,96]{1,2,0:T(8,128)(2,1)} %param.7) | data formatting | bytes 3145728 | tf_op args[2]
  16.8 0.0 collective-permute-done
  16.8 0.0 copy-done.2
  16.9 1.9 %pad_maximum_fusion = bf16[512,2048]{1,0:T(8,128)(2,1)} fusion(bf16[509,2048]{1,0:T(8,128)(2,1)S(1)} %bitcast.45, bf16[3,2048]{1,0:T(4,128)(2,1)S(1)} %collective-permute-done), kind=kLoop, calls=%fused_computation.17 | loop fusion | flops 4194304 | bytes 4194304 | tf_op jit(solution)/shard_map/concatenate | solution.py:45
  18.8 7.1 %reshape.93 = bf16[128,4,32,64]{3,2,1,0:T(8,128)(2,1)} reshape(bf16[512,2048]{1,0:T(8,128)(2,1)} %pad_maximum_fusion) | data formatting | bytes 4194304 | tf_op jit(solution)/shard_map/reshape | solution.py:27
  25.9 7.8 %fusion.12 = f32[128,32,96]{0,2,1:T(8,128)S(1)} fusion(bf16[32,4,64,96]{3,2,1,0:T(8,128)(2,1)} %bitcast.47, bf16[128,4,32,64]{3,2,1,0:T(8,128)(2,1)} %reshape.93), kind=kOutput, calls=%fused_computation.19 | convolution fusion | flops 201326592 | bytes 5242880 | tf_op jit(solution)/shard_map/jtgc,gtco->jgo/dot_general | solution.py:29
  33.7 0.0 copy-start.5
  33.7 1.1 multiply_reduce_fusion.1
  34.9 0.9 copy.15
  35.7 2.1 %copy.14 = f32[1,128,8,128]{3,1,2,0:T(8,128)} copy(f32[1,128,8,128]{1,3,2,0:T(8,128)} %bitcast.49) | data formatting | bytes 1048576 | tf_op jit(solution)/shard_map/reshape | solution.py:51
  37.8 1.2 multiply_convert_fusion.7
  39.0 1.9 %pad_maximum_fusion.1 = bf16[2,128,8,128]{3,1,2,0:T(8,128)(2,1)} fusion(bf16[1,128,8,128]{3,1,2,0:T(8,128)(2,1)} %copy.15, bf16[1,128,8,128]{3,1,2,0:T(8,128)(2,1)S(1)} %multiply_convert_fusion.7), kind=kLoop, calls=%fused_computation.27 | loop fusion | flops 262144 | bytes 1048576 | tf_op jit(solution)/shard_map/stack | solution.py:62
  40.9 0.0 all-gather.2.cloned.1.call-update
  40.9 0.2 iota_compare_fusion
  41.2 2.0 %copy.16 = f32[128,8,128]{2,0,1:T(8,128)} copy(f32[128,8,128]{0,2,1:T(8,128)} %bitcast.48) | data formatting | bytes 1048576 | tf_op jit(solution)/shard_map/reshape | solution.py:48
  43.2 60.8 %all-gather.2.cloned.1.call-done = bf16[2,2048,8,128]{3,1,2,0:T(8,128)(2,1)} async-done(((bf16[2,128,8,128]{3,1,2,0:T(8,128)(2,1)}), bf16[2,2048,8,128]{3,1,2,0:T(8,128)(2,1)}) %all-gather.2.cloned.1.call-update) | async-done | bytes 8388624 | tf_op jit(solution)/shard_map/all_gather | solution.py:63
  104.0 0.0 copy-done.5
  104.0 0.0 copy-start.4
  104.0 8.3 %fusion = (f32[8,128]{1,0:T(8,128)S(1)}, f32[8,128,2048]{2,1,0:T(8,128)}) fusion(f32[8]{0:T(128)S(1)} %copy-done.5, pred[128,2048]{1,0:T(8,128)(4,1)S(1)} %iota_compare_fusion, bf16[2,2048,8,128]{3,1,2,0:T(8,128)(2,1)} %all-gather.2.cloned.1.call-done, f32[128,8,128]{2,0,1:T(8,128)} %copy.16, f32[128,8]{0,1:T(8,128)S(1)} %add_rsqrt_fusion), kind=kOutput, calls=%fused_computation.1 | convolution fusion | flops 545520640 | bytes 13377568 | tf_op jit(solution)/shard_map/jsg,isg->sji/dot_general | solution.py:66
  112.3 0.0 copy-done.4
  112.3 0.0 copy-start.3
  112.3 5.8 %fusion.23 = bf16[128,8,128]{0,2,1:T(8,128)(2,1)S(1)} fusion(f32[8,128,2048]{2,1,0:T(8,128)} %get-tuple-element.10, f32[8]{0:T(128)S(1)} %copy-done.5, pred[128,2048]{1,0:T(8,128)(4,1)S(1)} %iota_compare_fusion, bf16[2,2048,8,128]{3,1,2,0:T(8,128)(2,1)S(1)} %copy-done.4, f32[128,8]{0,1:T(8,128)S(1)} %bitcast.54), kind=kOutput, calls=%fused_computation.25 | convolution fusion | flops 545521664 | bytes 13111808 | tf_op jit(solution)/shard_map/hqk,khd->qhd/dot_general | solution.py:77
  118.1 0.0 copy-done.3
  118.1 2.7 %convolution_bitcast_fusion = f32[128,32,256]{2,0,1:T(8,128)} fusion(bf16[128,32,32]{0,2,1:T(8,128)(2,1)S(1)} %bitcast.51, bf16[32,32,256]{2,1,0:T(8,128)(2,1)S(1)} %copy-done.3), kind=kOutput, calls=%fused_computation.15 | convolution fusion | flops 67108864 | bytes 4980736 | tf_op jit(solution)/shard_map/jgc,gcu->jgu/dot_general | solution.py:85
  120.8 5.6 %copy.18 = f32[128,32,256]{0,2,1:T(8,128)} copy(f32[128,32,256]{2,0,1:T(8,128)} %convolution_bitcast_fusion) | data formatting | bytes 8388608 | tf_op jit(solution)/shard_map/jgc,gcu->jgu/transpose | solution.py:85
  126.4 9.1 %copy.19 = f32[128,4,32,64]{3,2,1,0:T(8,128)} copy(f32[128,4,32,64]{0,3,1,2:T(8,128)} %bitcast.46) | data formatting | bytes 8388608 | tf_op jit(solution)/shard_map/transpose | solution.py:90
  135.5 7.8 %reshape.99 = f32[512,2048]{1,0:T(8,128)} reshape(f32[128,4,32,64]{3,2,1,0:T(8,128)} %copy.19) | data formatting | bytes 8388608 | tf_op jit(solution)/shard_map/reshape | solution.py:91
  143.3 0.0 copy-start.1
  143.3 3.0 %multiply_reduce_fusion = f32[512]{0:T(512)S(1)} fusion(f32[512,2048]{1,0:T(8,128)} %reshape.99, bf16[512,2048]{1,0:T(8,128)(2,1)S(1)} %copy-done.2), kind=kLoop, calls=%fused_computation.10 | loop fusion | flops 4193792 | bytes 6293504 | tf_op jit(solution)/shard_map/reduce_sum | solution.py:94
  146.3 0.0 copy-done
  146.3 0.5 copy-done.1
  146.8 1.5 fusion.19
  (7 shorter events, 0.1 us)
Async XLA Ops:
  6.5 139.8 %copy-start = (bf16[256,2048]{1,0:T(8,128)(2,1)S(1)}, bf16[256,2048]{1,0:T(8,128)(2,1)}, u32[]{:S(2)}) copy-start(bf16[256,2048]{1,0:T(8,128)(2,1)} %param.6) | copy-start | bytes 3145732
  6.5 10.3 %copy-start.2 = (bf16[512,2048]{1,0:T(8,128)(2,1)S(1)}, bf16[512,2048]{1,0:T(8,128)(2,1)}, u32[]{:S(2)}) copy-start(bf16[512,2048]{1,0:T(8,128)(2,1)} %param.5) | copy-start | bytes 6291460
  6.5 97.4 %all-gather.2.cloned.1.call-start = ((), (), s32[]{:S(2)}) async-start(), calls=%async_computation | async-start | bytes 8912896 | tf_op jit(solution)/shard_map/all_gather | solution.py:63
  7.5 9.4 %collective-permute-start = (bf16[3,2048]{1,0:T(4,128)(2,1)S(1)}, bf16[3,2048]{1,0:T(4,128)(2,1)S(1)}, u32[]{:S(2)}, u32[]{:S(2)}) collective-permute-start(bf16[3,2048]{1,0:T(4,128)(2,1)S(1)} %slice.22), channel_id=1, source_target_pairs={{0,1},{1,2},{2,3},{3,4},{4,5},{5,6},{6,7},{7,8},{8,9},{9,10},{10,1... | collective-permute-start | bytes 36872 | tf_op jit(solution)/shard_map/ppermute | solution.py:12
  33.7 70.3 %copy-start.5 = (f32[8]{0:T(128)S(1)}, f32[8]{0:T(128)}, u32[]{:S(2)}) copy-start(f32[8]{0:T(128)} %param.8) | copy-start | bytes 100
  104.0 8.3 %copy-start.4 = (bf16[2,2048,8,128]{3,1,2,0:T(8,128)(2,1)S(1)}, bf16[2,2048,8,128]{3,1,2,0:T(8,128)(2,1)}, u32[]{:S(2)}) copy-start(bf16[2,2048,8,128]{3,1,2,0:T(8,128)(2,1)} %all-gather.2.cloned.1.call-done) | copy-start | bytes 25165828
  112.3 5.9 %copy-start.3 = (bf16[32,32,256]{2,1,0:T(8,128)(2,1)S(1)}, bf16[32,32,256]{2,1,0:T(8,128)(2,1)}, u32[]{:S(2)}) copy-start(bf16[32,32,256]{2,1,0:T(8,128)(2,1)} %param.9) | copy-start | bytes 1572868
  143.3 3.4 %copy-start.1 = (f32[512,2048]{1,0:T(8,128)S(1)}, f32[512,2048]{1,0:T(8,128)}, u32[]{:S(2)}) copy-start(f32[512,2048]{1,0:T(8,128)} %reshape.99) | copy-start | bytes 12582916
Sparse Core Ops, SparseCore 0:
  41.0 62.9 all-gather.1
where the time goes:
time: 156 us; the launch traced here: 155 us
  waiting for transfers between devices  60.8 us (39%)
  local copies, waits for them, and re-layouts  39.9 us (26%)
  matrix products  26.1 us (17%)
  between operations  13.5 us (9%)
  other arithmetic  9.4 us (6%)
  starting transfers between devices  5.51 us (4%)
    all_gather x1, waiting for transfers between devices, on_device(): gathered = lax.all_gather(stacked, 'seq', axis=1, tiled=True)  60.8 us
    transpose x1, local copies, waits for them, and re-layouts, on_device(): upsampled = upsampled.reshape(tokens_here, groups, SHORTEN, group_width)....  9.14 us
    dot_general x1, matrix products, on_device(): jnp.einsum('jsg,isg->sji', queries, all_keys, preferred_element_type=jnp....  8.29 us
    reshape x1, local copies, waits for them, and re-layouts, on_device(): upsampled = upsampled.reshape(tokens_here, groups, SHORTEN, group_width)....  7.82 us
    dot_general x1, matrix products, shorten(): jnp.einsum('jtgc,gtco->jgo', windows, kernel, preferred_element_type=jnp....  7.76 us
    reshape x1, local copies, waits for them, and re-layouts, shorten(): shifted.reshape(byte_rows // SHORTEN, SHORTEN, groups, model_width // gro...  7.08 us
    dot_general x1, matrix products, on_device(): jnp.einsum('hqk,khd->qhd', softmax_shares.astype(jnp.bfloat16), all_value...  5.85 us
    transpose x1, local copies, waits for them, and re-layouts, on_device(): jnp.einsum('jgc,gcu->jgu', attended, widening_filter, preferred_element_t...  5.56 us
  transfers between devices with their start and end apart: 2, of which 1 were waited for; matrix products, arithmetic and copies ran while one was open for 4% of the time, Pallas kernels for 0%

commit v1 on v0

--- a/solution.py
+++ b/solution.py
@@ -4,6 +4,12 @@
 from jax.sharding import PartitionSpec as P
 
 SHORTEN = 4
+
+
+def in_order(blocks, dim):
+    blocks = jnp.moveaxis(blocks, 0, dim)
+    lengths = blocks.shape
+    return blocks.reshape(*lengths[:dim], lengths[dim] * lengths[dim + 1], *lengths[dim + 2 :])
 
 
 def shifted_2(array, axis, by):
@@ -60,7 +66,19 @@
     sharpness_vertical = sharpness_factor[:, None, None]
     query_pos = first_token + jnp.arange(tokens_here, dtype=jnp.int32)
     stacked = jnp.stack([key_unit, values], 0)
-    gathered = lax.all_gather(stacked, "seq", axis=1, tiled=True)
+    length = lax.axis_size("seq")
+    pairs_2 = [(i_2, (i_2 + 1) % length) for i_2 in range(length)]
+    back = [(b, a) for a, b in pairs_2]
+    lower, upper = ([], [])
+    for step in range(length - 1):
+        if step % 2 == 0:
+            lower.append(lax.ppermute(lower[-1] if lower else stacked, "seq", pairs_2))
+        else:
+            upper.append(lax.ppermute(upper[-1] if upper else stacked, "seq", back))
+    pieces = jnp.stack([*lower[::-1], stacked, *upper])
+    shift = lax.axis_index("seq") - len(lower)
+    pieces = pieces[(jnp.arange(length) - shift) % length]
+    gathered = in_order(pieces, 1)
     all_keys, all_values = (gathered[0], gathered[1])
     similarity_matrix = (
         jnp.einsum("jsg,isg->sji", queries, all_keys, preferred_element_type=jnp.float32)

time: 156 us -> 206 us (1.32)
  the two profiles are of different devices: /device:TPU:1 before, /device:TPU:46 now
where the time goes in v1:
time: 206 us; the launch traced here: 204 us
  local copies, waits for them, and re-layouts  92 us (45%)
  waiting for transfers between devices  59.4 us (29%)
  starting transfers between devices  25.4 us (12%)
  matrix products  21.1 us (10%)
  other arithmetic  6.4 us (3%)
    ppermute x8, waiting for transfers between devices, on_device(): lower.append(lax.ppermute(lower[-1] if lower else stacked, 'seq', pairs_2))  59.2 us
    unnamed x43, local copies, waits for them, and re-layouts  26.2 us
    ppermute x7, starting transfers between devices, on_device(): upper.append(lax.ppermute(upper[-1] if upper else stacked, 'seq', back))  20.9 us
    slice x3, local copies, waits for them, and re-layouts, on_device(): all_keys, all_values = (gathered[0], gathered[1])  19.4 us
    transpose x1, local copies, waits for them, and re-layouts, on_device(): upsampled = upsampled.reshape(tokens_here, groups, SHORTEN, group_width)....  9.19 us
    gather x1, local copies, waits for them, and re-layouts, on_device(): pieces = pieces[(jnp.arange(length) - shift) % length]  8.16 us
    reshape x1, local copies, waits for them, and re-layouts, on_device(): upsampled = upsampled.reshape(tokens_here, groups, SHORTEN, group_width)....  7.97 us
    dot_general x1, matrix products, shorten(): jnp.einsum('jtgc,gtco->jgo', windows, kernel, preferred_element_type=jnp....  7.77 us
  transfers between devices with their start and end apart: 16, of which 9 were waited for; matrix products, arithmetic and copies ran while one was open for 14% of the time, Pallas kernels for 0%

profile of v1, /device:TPU:46, one launch (start us, length us, event | category | flops | bytes accessed | tf_op | source)
XLA Modules:
  0.0 204.5 jit_solution(8699482430355987684)
XLA Ops:
  0.0 0.9 slice.24
  0.9 1.7 collective-permute-start
  2.6 3.9 %copy.11 = bf16[32,256,96]{2,1,0:T(8,128)(2,1)} copy(bf16[32,256,96]{1,2,0:T(8,128)(2,1)} %param.7) | data formatting | bytes 3145728 | tf_op args[2]
  6.5 0.0 collective-permute-done
  6.5 2.1 %pad_maximum_fusion = bf16[512,2048]{1,0:T(8,128)(2,1)S(1)} fusion(bf16[509,2048]{1,0:T(8,128)(2,1)} %bitcast.74, bf16[3,2048]{1,0:T(4,128)(2,1)S(1)} %collective-permute-done), kind=kLoop, calls=%fused_computation.15 | loop fusion | flops 4194304 | bytes 4194304 | tf_op jit(solution)/shard_map/concatenate | solution.py:51
  8.6 5.3 %reshape.147 = bf16[128,4,32,64]{3,2,1,0:T(8,128)(2,1)} reshape(bf16[512,2048]{1,0:T(8,128)(2,1)S(1)} %pad_maximum_fusion) | data formatting | bytes 4194304 | tf_op jit(solution)/shard_map/reshape | solution.py:33
  13.9 7.8 %fusion.11 = f32[128,32,96]{0,2,1:T(8,128)S(1)} fusion(bf16[32,4,64,96]{3,2,1,0:T(8,128)(2,1)} %bitcast.79, bf16[128,4,32,64]{3,2,1,0:T(8,128)(2,1)} %reshape.147), kind=kOutput, calls=%fused_computation.17 | convolution fusion | flops 201326592 | bytes 5242880 | tf_op jit(solution)/shard_map/jtgc,gtco->jgo/dot_general | solution.py:35
  21.7 0.3 multiply_reduce_fusion.1
  22.1 0.1 pad_maximum_fusion.1
  22.2 2.7 %collective-permute-start.1 = (bf16[2,128,8,128]{1,3,2,0:T(8,128)(2,1)S(1)}, bf16[2,128,8,128]{1,3,2,0:T(8,128)(2,1)S(1)}, u32[]{:S(2)}, u32[]{:S(2)}) collective-permute-start(bf16[2,128,8,128]{1,3,2,0:T(8,128)(2,1)S(1)} %pad_maximum_fusion.1), channel_id=1, source_target_pairs={{0,1},{1,2},{2,3},{3,4},{4,5},{5,6},{6,7},{7,8},{8,9},{9,10},{10,1... | collective-permute-start | bytes 1572872 | tf_op jit(solution)/shard_map/ppermute | solution.py:75
  24.8 12.2 %collective-permute-done.1 = bf16[2,128,8,128]{1,3,2,0:T(8,128)(2,1)S(1)} collective-permute-done((bf16[2,128,8,128]{1,3,2,0:T(8,128)(2,1)S(1)}, bf16[2,128,8,128]{1,3,2,0:T(8,128)(2,1)S(1)}, u32[]{:S(2)}, u32[]{:S(2)}) %collective-permute-start.1) | collective-permute-done | bytes 524320 | tf_op jit(solution)/shard_map/ppermute | solution.py:75
  37.1 3.0 %collective-permute-start.9 = (bf16[2,128,8,128]{1,3,2,0:T(8,128)(2,1)S(1)}, bf16[2,128,8,128]{1,3,2,0:T(8,128)(2,1)S(1)}, u32[]{:S(2)}, u32[]{:S(2)}) collective-permute-start(bf16[2,128,8,128]{1,3,2,0:T(8,128)(2,1)S(1)} %pad_maximum_fusion.1), channel_id=1, source_target_pairs={{1,0},{2,1},{3,2},{4,3},{5,4},{6,5},{7,6},{8,7},{9,8},{10,9},{11,1... | collective-permute-start | bytes 1572872 | tf_op jit(solution)/shard_map/ppermute | solution.py:77
  40.0 6.9 %collective-permute-done.2 = bf16[2,128,8,128]{1,3,2,0:T(8,128)(2,1)S(1)} collective-permute-done((bf16[2,128,8,128]{1,3,2,0:T(8,128)(2,1)S(1)}, bf16[2,128,8,128]{1,3,2,0:T(8,128)(2,1)S(1)}, u32[]{:S(2)}, u32[]{:S(2)}) %collective-permute-start.2) | collective-permute-done | bytes 524320 | tf_op jit(solution)/shard_map/ppermute | solution.py:75
  46.9 0.0 collective-permute-start.3
  46.9 0.0 collective-permute-done.9
  46.9 3.0 %collective-permute-start.10 = (bf16[2,128,8,128]{1,3,2,0:T(8,128)(2,1)S(1)}, bf16[2,128,8,128]{1,3,2,0:T(8,128)(2,1)S(1)}, u32[]{:S(2)}, u32[]{:S(2)}) collective-permute-start(bf16[2,128,8,128]{1,3,2,0:T(8,128)(2,1)S(1)} %collective-permute-done.9), channel_id=1, source_target_pairs={{1,0},{2,1},{3,2},{4,3},{5,4},{6,5},{7,6},{8,7},{9,8},{10,9},{11,1... | collective-permute-start | bytes 1572872 | tf_op jit(solution)/shard_map/ppermute | solution.py:77
  49.9 6.9 %collective-permute-done.3 = bf16[2,128,8,128]{1,3,2,0:T(8,128)(2,1)S(1)} collective-permute-done((bf16[2,128,8,128]{1,3,2,0:T(8,128)(2,1)S(1)}, bf16[2,128,8,128]{1,3,2,0:T(8,128)(2,1)S(1)}, u32[]{:S(2)}, u32[]{:S(2)}) %collective-permute-start.3) | collective-permute-done | bytes 524320 | tf_op jit(solution)/shard_map/ppermute | solution.py:75
  56.7 0.0 collective-permute-start.4
  56.7 0.0 collective-permute-done.10
  56.8 2.9 %collective-permute-start.11 = (bf16[2,128,8,128]{1,3,2,0:T(8,128)(2,1)S(1)}, bf16[2,128,8,128]{1,3,2,0:T(8,128)(2,1)S(1)}, u32[]{:S(2)}, u32[]{:S(2)}) collective-permute-start(bf16[2,128,8,128]{1,3,2,0:T(8,128)(2,1)S(1)} %collective-permute-done.10), channel_id=1, source_target_pairs={{1,0},{2,1},{3,2},{4,3},{5,4},{6,5},{7,6},{8,7},{9,8},{10,9},{11,1... | collective-permute-start | bytes 1572872 | tf_op jit(solution)/shard_map/ppermute | solution.py:77
  59.7 6.8 %collective-permute-done.4 = bf16[2,128,8,128]{1,3,2,0:T(8,128)(2,1)S(1)} collective-permute-done((bf16[2,128,8,128]{1,3,2,0:T(8,128)(2,1)S(1)}, bf16[2,128,8,128]{1,3,2,0:T(8,128)(2,1)S(1)}, u32[]{:S(2)}, u32[]{:S(2)}) %collective-permute-start.4) | collective-permute-done | bytes 524320 | tf_op jit(solution)/shard_map/ppermute | solution.py:75
  66.6 2.9 %collective-permute-start.12 = (bf16[2,128,8,128]{1,3,2,0:T(8,128)(2,1)S(1)}, bf16[2,128,8,128]{1,3,2,0:T(8,128)(2,1)}, u32[]{:S(2)}, u32[]{:S(2)}) collective-permute-start(bf16[2,128,8,128]{1,3,2,0:T(8,128)(2,1)S(1)} %collective-permute-done.11), channel_id=1, source_target_pairs={{1,0},{2,1},{3,2},{4,3},{5,4},{6,5},{7,6},{8,7},{9,8},{10,9},{11,1... | collective-permute-start | bytes 1572872 | tf_op jit(solution)/shard_map/ppermute | solution.py:77
  69.5 6.8 %collective-permute-done.5 = bf16[2,128,8,128]{1,3,2,0:T(8,128)(2,1)S(1)} collective-permute-done((bf16[2,128,8,128]{1,3,2,0:T(8,128)(2,1)S(1)}, bf16[2,128,8,128]{1,3,2,0:T(8,128)(2,1)S(1)}, u32[]{:S(2)}, u32[]{:S(2)}) %collective-permute-start.5) | collective-permute-done | bytes 524320 | tf_op jit(solution)/shard_map/ppermute | solution.py:75
  76.4 0.0 collective-permute-start.6
  76.4 0.0 collective-permute-done.12
  76.4 3.1 %collective-permute-start.13 = (bf16[2,128,8,128]{1,3,2,0:T(8,128)(2,1)}, bf16[2,128,8,128]{1,3,2,0:T(8,128)(2,1)}, u32[]{:S(2)}, u32[]{:S(2)}) collective-permute-start(bf16[2,128,8,128]{1,3,2,0:T(8,128)(2,1)} %collective-permute-done.12), channel_id=1, source_target_pairs={{1,0},{2,1},{3,2},{4,3},{5,4},{6,5},{7,6},{8,7},{9,8},{10,9},{11,1... | collective-permute-start | bytes 1572872 | tf_op jit(solution)/shard_map/ppermute | solution.py:77
  79.5 6.8 %collective-permute-done.6 = bf16[2,128,8,128]{1,3,2,0:T(8,128)(2,1)} collective-permute-done((bf16[2,128,8,128]{1,3,2,0:T(8,128)(2,1)S(1)}, bf16[2,128,8,128]{1,3,2,0:T(8,128)(2,1)}, u32[]{:S(2)}, u32[]{:S(2)}) %collective-permute-start.6) | collective-permute-done | bytes 524320 | tf_op jit(solution)/shard_map/ppermute | solution.py:75
  86.3 0.1 collective-permute-done.13
  86.5 3.1 %collective-permute-start.14 = (bf16[2,128,8,128]{1,3,2,0:T(8,128)(2,1)}, bf16[2,128,8,128]{1,3,2,0:T(8,128)(2,1)}, u32[]{:S(2)}, u32[]{:S(2)}) collective-permute-start(bf16[2,128,8,128]{1,3,2,0:T(8,128)(2,1)} %collective-permute-done.13), channel_id=1, source_target_pairs={{1,0},{2,1},{3,2},{4,3},{5,4},{6,5},{7,6},{8,7},{9,8},{10,9},{11,1... | collective-permute-start | bytes 1572872 | tf_op jit(solution)/shard_map/ppermute | solution.py:77
  89.6 6.8 %collective-permute-done.7 = bf16[2,128,8,128]{1,3,2,0:T(8,128)(2,1)} collective-permute-done((bf16[2,128,8,128]{1,3,2,0:T(8,128)(2,1)}, bf16[2,128,8,128]{1,3,2,0:T(8,128)(2,1)}, u32[]{:S(2)}, u32[]{:S(2)}) %collective-permute-start.7) | collective-permute-done | bytes 524320 | tf_op jit(solution)/shard_map/ppermute | solution.py:75
  96.4 0.2 iota_compare_fusion
  96.6 1.0 copy.14
  97.7 3.0 %collective-permute-start.15 = (bf16[2,128,8,128]{1,3,2,0:T(8,128)(2,1)}, bf16[2,128,8,128]{1,3,2,0:T(8,128)(2,1)S(1)}, u32[]{:S(2)}, u32[]{:S(2)}) collective-permute-start(bf16[2,128,8,128]{1,3,2,0:T(8,128)(2,1)} %collective-permute-done.14), channel_id=1, source_target_pairs={{1,0},{2,1},{3,2},{4,3},{5,4},{6,5},{7,6},{8,7},{9,8},{10,9},{11,1... | collective-permute-start | bytes 1572872 | tf_op jit(solution)/shard_map/ppermute | solution.py:77
  100.7 5.9 %collective-permute-done.8 = bf16[2,128,8,128]{1,3,2,0:T(8,128)(2,1)} collective-permute-done((bf16[2,128,8,128]{1,3,2,0:T(8,128)(2,1)}, bf16[2,128,8,128]{1,3,2,0:T(8,128)(2,1)}, u32[]{:S(2)}, u32[]{:S(2)}) %collective-permute-start.8) | collective-permute-done | bytes 524320 | tf_op jit(solution)/shard_map/ppermute | solution.py:75
  106.6 1.9 bitcast_dynamic-update-slice_fusion.15
  108.4 1.9 bitcast_dynamic-update-slice_fusion.14
  110.3 1.9 bitcast_dynamic-update-slice_fusion.13
  112.2 1.9 bitcast_dynamic-update-slice_fusion.12
  114.2 1.9 bitcast_dynamic-update-slice_fusion.11
  116.0 1.9 bitcast_dynamic-update-slice_fusion.10
  118.0 1.9 bitcast_dynamic-update-slice_fusion.9
  119.8 0.8 bitcast_dynamic-update-slice_fusion.8
  120.7 0.8 bitcast_dynamic-update-slice_fusion.7
  121.5 0.8 bitcast_dynamic-update-slice_fusion.6
  122.3 0.9 bitcast_dynamic-update-slice_fusion.5
  123.2 0.8 bitcast_dynamic-update-slice_fusion.4
  124.1 1.9 bitcast_dynamic-update-slice_fusion.3
  126.0 1.9 bitcast_dynamic-update-slice_fusion.2
  127.8 1.9 bitcast_dynamic-update-slice_fusion.1
  129.7 0.9 bitcast_dynamic-update-slice_fusion
  130.6 8.2 %gather_fusion = bf16[16,2,128,8,128]{2,4,3,1,0:T(8,128)(2,1)} fusion(bf16[16,2,128,8,128]{2,4,3,1,0:T(8,128)(2,1)} %bitcast_dynamic-update-slice_fusion, s32[1024]{0:T(1024)S(1)} %pad_clamp_fusion), kind=kCustom, calls=%fused_computation | custom fusion | bytes 16777280 | tf_op jit(solution)/shard_map/gather | solution.py:80
  138.8 6.0 %fusion.30 = (bf16[1,16,128,8,128]{2,4,3,0,1:T(8,128)(2,1)}, bf16[1,16,128,8,128]{2,4,3,0,1:T(8,128)(2,1)}) fusion(bf16[2,16,128,8,128]{2,4,3,0,1:T(8,128)(2,1)} %bitcast.73), kind=kLoop, calls=%fused_computation.60 | loop fusion | bytes 16777216 | tf_op jit(solution)/shard_map/slice | solution.py:82
  144.8 6.5 %copy.15 = bf16[1,16,128,8,128]{4,2,1,3,0:T(8,128)(2,1)} copy(bf16[1,16,128,8,128]{2,4,3,0,1:T(8,128)(2,1)} %get-tuple-element.7) | data formatting | bytes 8388608 | tf_op jit(solution)/shard_map/slice | solution.py:82
  151.3 6.9 %copy.13 = bf16[1,16,128,8,128]{2,1,4,3,0:T(8,128)(2,1)} copy(bf16[1,16,128,8,128]{2,4,3,0,1:T(8,128)(2,1)} %get-tuple-element.8) | data formatting | bytes 8388608 | tf_op jit(solution)/shard_map/slice | solution.py:82
  158.2 7.4 %squeeze.6 = bf16[2048,8,128]{0,2,1:T(8,128)(2,1)} reshape(bf16[1,16,128,8,128]{2,1,4,3,0:T(8,128)(2,1)} %copy.13) | data formatting | bytes 8388608 | tf_op jit(solution)/shard_map/squeeze | solution.py:82
  165.5 4.9 %fusion = (f32[8,128]{1,0:T(8,128)S(1)}, f32[8,128,2048]{2,1,0:T(8,128)S(1)}) fusion(f32[8]{0:T(128)S(1)} %copy-done.13, pred[128,2048]{1,0:T(8,128)(4,1)S(1)} %iota_compare_fusion, bf16[2048,8,128]{2,0,1:T(8,128)(2,1)} %bitcast.76, f32[128,8,128]{2,0,1:T(8,128)S(1)} %copy-done.12, f32[128,8]{0,1:T(8,128)S(1)} %add_rsqrt_fusion), kind=kOutput, calls=%fused_computation.2 | convolution fusion | flops 545520640 | bytes 13377568 | tf_op jit(solution)/shard_map/jsg,isg->sji/dot_general | solution.py:84
  170.5 0.0 copy-start.3
  170.5 2.0 fusion.22
  172.5 2.7 %convolution_bitcast_fusion = f32[128,32,256]{2,0,1:T(8,128)} fusion(bf16[128,32,32]{0,2,1:T(8,128)(2,1)S(1)} %bitcast.82, bf16[32,32,256]{2,1,0:T(8,128)(2,1)S(1)} %copy-done.3), kind=kOutput, calls=%fused_computation.13 | convolution fusion | flops 67108864 | bytes 4980736 | tf_op jit(solution)/shard_map/jgc,gcu->jgu/dot_general | solution.py:103
  175.3 5.6 %copy.16 = f32[128,32,256]{0,2,1:T(8,128)} copy(f32[128,32,256]{2,0,1:T(8,128)} %convolution_bitcast_fusion) | data formatting | bytes 8388608 | tf_op jit(solution)/shard_map/jgc,gcu->jgu/transpose | solution.py:103
  180.8 9.2 %copy.17 = f32[128,4,32,64]{3,2,1,0:T(8,128)} copy(f32[128,4,32,64]{0,3,1,2:T(8,128)} %bitcast.75) | data formatting | bytes 8388608 | tf_op jit(solution)/shard_map/transpose | solution.py:108
  190.0 8.0 %reshape.153 = f32[512,2048]{1,0:T(8,128)} reshape(f32[128,4,32,64]{3,2,1,0:T(8,128)} %copy.17) | data formatting | bytes 8388608 | tf_op jit(solution)/shard_map/reshape | solution.py:109
  198.0 2.8 %multiply_reduce_fusion = f32[512]{0:T(512)S(1)} fusion(f32[512,2048]{1,0:T(8,128)} %reshape.153, bf16[512,2048]{1,0:T(8,128)(2,1)S(1)} %copy-done.1), kind=kLoop, calls=%fused_computation.8 | loop fusion | flops 4193792 | bytes 6293504 | tf_op jit(solution)/shard_map/reduce_sum | solution.py:112
  200.8 3.7 %fusion.18 = bf16[512,256]{1,0:T(8,128)(2,1)} fusion(bf16[256,2048]{1,0:T(8,128)(2,1)S(1)} %copy-done, f32[512,2048]{1,0:T(8,128)} %reshape.153, bf16[512,2048]{1,0:T(8,128)(2,1)S(1)} %copy-done.1, f32[512]{0:T(512)S(1)} %add_rsqrt_fusion.2), kind=kOutput, calls=%fused_computation.20 | convolution fusion | flops 541327360 | bytes 7604224 | tf_op jit(solution)/shard_map/dot_general | solution.py:115
  (44 shorter events, 0.2 us)
Async XLA Ops:
  0.0 200.8 %copy-start = (bf16[256,2048]{1,0:T(8,128)(2,1)S(1)}, bf16[256,2048]{1,0:T(8,128)(2,1)}, u32[]{:S(2)}) copy-start(bf16[256,2048]{1,0:T(8,128)(2,1)} %param.6) | copy-start | bytes 3145732
  0.9 5.6 %collective-permute-start = (bf16[3,2048]{1,0:T(4,128)(2,1)S(1)}, bf16[3,2048]{1,0:T(4,128)(2,1)S(1)}, u32[]{:S(2)}, u32[]{:S(2)}) collective-permute-start(bf16[3,2048]{1,0:T(4,128)(2,1)S(1)} %slice.24), channel_id=1, source_target_pairs={{0,1},{1,2},{2,3},{3,4},{4,5},{5,6},{6,7},{7,8},{8,9},{9,10},{10,1... | collective-permute-start | bytes 36872 | tf_op jit(solution)/shard_map/ppermute | solution.py:18
  22.2 14.9 %collective-permute-start.1 = (bf16[2,128,8,128]{1,3,2,0:T(8,128)(2,1)S(1)}, bf16[2,128,8,128]{1,3,2,0:T(8,128)(2,1)S(1)}, u32[]{:S(2)}, u32[]{:S(2)}) collective-permute-start(bf16[2,128,8,128]{1,3,2,0:T(8,128)(2,1)S(1)} %pad_maximum_fusion.1), channel_id=1, source_target_pairs={{0,1},{1,2},{2,3},{3,4},{4,5},{5,6},{6,7},{7,8},{8,9},{9,10},{10,1... | collective-permute-start | bytes 1572872 | tf_op jit(solution)/shard_map/ppermute | solution.py:75
  37.1 9.8 %collective-permute-start.2 = (bf16[2,128,8,128]{1,3,2,0:T(8,128)(2,1)S(1)}, bf16[2,128,8,128]{1,3,2,0:T(8,128)(2,1)S(1)}, u32[]{:S(2)}, u32[]{:S(2)}) collective-permute-start(bf16[2,128,8,128]{1,3,2,0:T(8,128)(2,1)S(1)} %collective-permute-done.1), channel_id=1, source_target_pairs={{0,1},{1,2},{2,3},{3,4},{4,5},{5,6},{6,7},{7,8},{8,9},{9,10},{10,1... | collective-permute-start | bytes 1572872 | tf_op jit(solution)/shard_map/ppermute | solution.py:75
  37.1 9.8 %collective-permute-start.9 = (bf16[2,128,8,128]{1,3,2,0:T(8,128)(2,1)S(1)}, bf16[2,128,8,128]{1,3,2,0:T(8,128)(2,1)S(1)}, u32[]{:S(2)}, u32[]{:S(2)}) collective-permute-start(bf16[2,128,8,128]{1,3,2,0:T(8,128)(2,1)S(1)} %pad_maximum_fusion.1), channel_id=1, source_target_pairs={{1,0},{2,1},{3,2},{4,3},{5,4},{6,5},{7,6},{8,7},{9,8},{10,9},{11,1... | collective-permute-start | bytes 1572872 | tf_op jit(solution)/shard_map/ppermute | solution.py:77
  46.9 9.8 %copy-start.4 = (bf16[2,128,8,128]{1,3,2,0:T(8,128)(2,1)}, bf16[2,128,8,128]{1,3,2,0:T(8,128)(2,1)S(1)}, u32[]{:S(2)}) copy-start(bf16[2,128,8,128]{1,3,2,0:T(8,128)(2,1)S(1)} %collective-permute-done.2) | copy-start | bytes 1572868
  46.9 9.8 %collective-permute-start.3 = (bf16[2,128,8,128]{1,3,2,0:T(8,128)(2,1)S(1)}, bf16[2,128,8,128]{1,3,2,0:T(8,128)(2,1)S(1)}, u32[]{:S(2)}, u32[]{:S(2)}) collective-permute-start(bf16[2,128,8,128]{1,3,2,0:T(8,128)(2,1)S(1)} %collective-permute-done.2), channel_id=1, source_target_pairs={{0,1},{1,2},{2,3},{3,4},{4,5},{5,6},{6,7},{7,8},{8,9},{9,10},{10,1... | collective-permute-start | bytes 1572872 | tf_op jit(solution)/shard_map/ppermute | solution.py:75
  46.9 9.8 %collective-permute-start.10 = (bf16[2,128,8,128]{1,3,2,0:T(8,128)(2,1)S(1)}, bf16[2,128,8,128]{1,3,2,0:T(8,128)(2,1)S(1)}, u32[]{:S(2)}, u32[]{:S(2)}) collective-permute-start(bf16[2,128,8,128]{1,3,2,0:T(8,128)(2,1)S(1)} %collective-permute-done.9), channel_id=1, source_target_pairs={{1,0},{2,1},{3,2},{4,3},{5,4},{6,5},{7,6},{8,7},{9,8},{10,9},{11,1... | collective-permute-start | bytes 1572872 | tf_op jit(solution)/shard_map/ppermute | solution.py:77
  56.7 9.8 %copy-start.7 = (bf16[2,128,8,128]{1,3,2,0:T(8,128)(2,1)}, bf16[2,128,8,128]{1,3,2,0:T(8,128)(2,1)S(1)}, u32[]{:S(2)}) copy-start(bf16[2,128,8,128]{1,3,2,0:T(8,128)(2,1)S(1)} %collective-permute-done.3) | copy-start | bytes 1572868
  56.7 9.8 %collective-permute-start.4 = (bf16[2,128,8,128]{1,3,2,0:T(8,128)(2,1)S(1)}, bf16[2,128,8,128]{1,3,2,0:T(8,128)(2,1)S(1)}, u32[]{:S(2)}, u32[]{:S(2)}) collective-permute-start(bf16[2,128,8,128]{1,3,2,0:T(8,128)(2,1)S(1)} %collective-permute-done.3), channel_id=1, source_target_pairs={{0,1},{1,2},{2,3},{3,4},{4,5},{5,6},{6,7},{7,8},{8,9},{9,10},{10,1... | collective-permute-start | bytes 1572872 | tf_op jit(solution)/shard_map/ppermute | solution.py:75
  56.7 3.0 %copy-start.5 = (bf16[2,128,8,128]{1,3,2,0:T(8,128)(2,1)}, bf16[2,128,8,128]{1,3,2,0:T(8,128)(2,1)S(1)}, u32[]{:S(2)}) copy-start(bf16[2,128,8,128]{1,3,2,0:T(8,128)(2,1)S(1)} %collective-permute-done.10) | copy-start | bytes 1572868
  56.8 9.8 %collective-permute-start.11 = (bf16[2,128,8,128]{1,3,2,0:T(8,128)(2,1)S(1)}, bf16[2,128,8,128]{1,3,2,0:T(8,128)(2,1)S(1)}, u32[]{:S(2)}, u32[]{:S(2)}) collective-permute-start(bf16[2,128,8,128]{1,3,2,0:T(8,128)(2,1)S(1)} %collective-permute-done.10), channel_id=1, source_target_pairs={{1,0},{2,1},{3,2},{4,3},{5,4},{6,5},{7,6},{8,7},{9,8},{10,9},{11,1... | collective-permute-start | bytes 1572872 | tf_op jit(solution)/shard_map/ppermute | solution.py:77
  66.5 9.8 %copy-start.10 = (bf16[2,128,8,128]{1,3,2,0:T(8,128)(2,1)}, bf16[2,128,8,128]{1,3,2,0:T(8,128)(2,1)S(1)}, u32[]{:S(2)}) copy-start(bf16[2,128,8,128]{1,3,2,0:T(8,128)(2,1)S(1)} %collective-permute-done.4) | copy-start | bytes 1572868
  66.5 9.8 %collective-permute-start.5 = (bf16[2,128,8,128]{1,3,2,0:T(8,128)(2,1)S(1)}, bf16[2,128,8,128]{1,3,2,0:T(8,128)(2,1)S(1)}, u32[]{:S(2)}, u32[]{:S(2)}) collective-permute-start(bf16[2,128,8,128]{1,3,2,0:T(8,128)(2,1)S(1)} %collective-permute-done.4), channel_id=1, source_target_pairs={{0,1},{1,2},{2,3},{3,4},{4,5},{5,6},{6,7},{7,8},{8,9},{9,10},{10,1... | collective-permute-start | bytes 1572872 | tf_op jit(solution)/shard_map/ppermute | solution.py:75
  66.6 3.0 %copy-start.8 = (bf16[2,128,8,128]{1,3,2,0:T(8,128)(2,1)}, bf16[2,128,8,128]{1,3,2,0:T(8,128)(2,1)S(1)}, u32[]{:S(2)}) copy-start(bf16[2,128,8,128]{1,3,2,0:T(8,128)(2,1)S(1)} %collective-permute-done.11) | copy-start | bytes 1572868
  66.6 9.8 %collective-permute-start.12 = (bf16[2,128,8,128]{1,3,2,0:T(8,128)(2,1)S(1)}, bf16[2,128,8,128]{1,3,2,0:T(8,128)(2,1)}, u32[]{:S(2)}, u32[]{:S(2)}) collective-permute-start(bf16[2,128,8,128]{1,3,2,0:T(8,128)(2,1)S(1)} %collective-permute-done.11), channel_id=1, source_target_pairs={{1,0},{2,1},{3,2},{4,3},{5,4},{6,5},{7,6},{8,7},{9,8},{10,9},{11,1... | collective-permute-start | bytes 1572872 | tf_op jit(solution)/shard_map/ppermute | solution.py:77
  76.4 3.1 %copy-start.11 = (bf16[2,128,8,128]{1,3,2,0:T(8,128)(2,1)}, bf16[2,128,8,128]{1,3,2,0:T(8,128)(2,1)S(1)}, u32[]{:S(2)}) copy-start(bf16[2,128,8,128]{1,3,2,0:T(8,128)(2,1)S(1)} %collective-permute-done.5) | copy-start | bytes 1572868
  76.4 9.9 %collective-permute-start.6 = (bf16[2,128,8,128]{1,3,2,0:T(8,128)(2,1)S(1)}, bf16[2,128,8,128]{1,3,2,0:T(8,128)(2,1)}, u32[]{:S(2)}, u32[]{:S(2)}) collective-permute-start(bf16[2,128,8,128]{1,3,2,0:T(8,128)(2,1)S(1)} %collective-permute-done.5), channel_id=1, source_target_pairs={{0,1},{1,2},{2,3},{3,4},{4,5},{5,6},{6,7},{7,8},{8,9},{9,10},{10,1... | collective-permute-start | bytes 1572872 | tf_op jit(solution)/shard_map/ppermute | solution.py:75
  76.4 10.1 %collective-permute-start.13 = (bf16[2,128,8,128]{1,3,2,0:T(8,128)(2,1)}, bf16[2,128,8,128]{1,3,2,0:T(8,128)(2,1)}, u32[]{:S(2)}, u32[]{:S(2)}) collective-permute-start(bf16[2,128,8,128]{1,3,2,0:T(8,128)(2,1)} %collective-permute-done.12), channel_id=1, source_target_pairs={{1,0},{2,1},{3,2},{4,3},{5,4},{6,5},{7,6},{8,7},{9,8},{10,9},{11,1... | collective-permute-start | bytes 1572872 | tf_op jit(solution)/shard_map/ppermute | solution.py:77
  86.3 10.1 %collective-permute-start.7 = (bf16[2,128,8,128]{1,3,2,0:T(8,128)(2,1)}, bf16[2,128,8,128]{1,3,2,0:T(8,128)(2,1)}, u32[]{:S(2)}, u32[]{:S(2)}) collective-permute-start(bf16[2,128,8,128]{1,3,2,0:T(8,128)(2,1)} %collective-permute-done.6), channel_id=1, source_target_pairs={{0,1},{1,2},{2,3},{3,4},{4,5},{5,6},{6,7},{7,8},{8,9},{9,10},{10,1... | collective-permute-start | bytes 1572872 | tf_op jit(solution)/shard_map/ppermute | solution.py:75
  86.5 11.2 %collective-permute-start.14 = (bf16[2,128,8,128]{1,3,2,0:T(8,128)(2,1)}, bf16[2,128,8,128]{1,3,2,0:T(8,128)(2,1)}, u32[]{:S(2)}, u32[]{:S(2)}) collective-permute-start(bf16[2,128,8,128]{1,3,2,0:T(8,128)(2,1)} %collective-permute-done.13), channel_id=1, source_target_pairs={{1,0},{2,1},{3,2},{4,3},{5,4},{6,5},{7,6},{8,7},{9,8},{10,9},{11,1... | collective-permute-start | bytes 1572872 | tf_op jit(solution)/shard_map/ppermute | solution.py:77
  96.4 10.1 %collective-permute-start.8 = (bf16[2,128,8,128]{1,3,2,0:T(8,128)(2,1)}, bf16[2,128,8,128]{1,3,2,0:T(8,128)(2,1)}, u32[]{:S(2)}, u32[]{:S(2)}) collective-permute-start(bf16[2,128,8,128]{1,3,2,0:T(8,128)(2,1)} %collective-permute-done.7), channel_id=1, source_target_pairs={{0,1},{1,2},{2,3},{3,4},{4,5},{5,6},{6,7},{7,8},{8,9},{9,10},{10,1... | collective-permute-start | bytes 1572872 | tf_op jit(solution)/shard_map/ppermute | solution.py:75
  97.6 24.7 %copy-start.6 = (bf16[2,128,8,128]{1,3,2,0:T(8,128)(2,1)S(1)}, bf16[2,128,8,128]{1,3,2,0:T(8,128)(2,1)}, u32[]{:S(2)}) copy-start(bf16[2,128,8,128]{1,3,2,0:T(8,128)(2,1)} %copy-done.5) | copy-start | bytes 1572868
  97.7 25.6 %copy-start.9 = (bf16[2,128,8,128]{1,3,2,0:T(8,128)(2,1)S(1)}, bf16[2,128,8,128]{1,3,2,0:T(8,128)(2,1)}, u32[]{:S(2)}) copy-start(bf16[2,128,8,128]{1,3,2,0:T(8,128)(2,1)} %copy-done.8) | copy-start | bytes 1572868
  97.7 32.0 %collective-permute-start.15 = (bf16[2,128,8,128]{1,3,2,0:T(8,128)(2,1)}, bf16[2,128,8,128]{1,3,2,0:T(8,128)(2,1)S(1)}, u32[]{:S(2)}, u32[]{:S(2)}) collective-permute-start(bf16[2,128,8,128]{1,3,2,0:T(8,128)(2,1)} %collective-permute-done.14), channel_id=1, source_target_pairs={{1,0},{2,1},{3,2},{4,3},{5,4},{6,5},{7,6},{8,7},{9,8},{10,9},{11,1... | collective-permute-start | bytes 1572872 | tf_op jit(solution)/shard_map/ppermute | solution.py:77
  151.3 14.3 %copy-start.12 = (f32[128,8,128]{2,0,1:T(8,128)S(1)}, f32[128,8,128]{2,0,1:T(8,128)}, u32[]{:S(2)}) copy-start(f32[128,8,128]{2,0,1:T(8,128)} %copy.14) | copy-start | bytes 1572868
  151.3 14.3 %copy-start.13 = (f32[8]{0:T(128)S(1)}, f32[8]{0:T(128)}, u32[]{:S(2)}) copy-start(f32[8]{0:T(128)} %param.8) | copy-start | bytes 100
  165.5 4.9 %copy-start.2 = (bf16[2048,8,128]{0,2,1:T(8,128)(2,1)S(1)}, bf16[2048,8,128]{0,2,1:T(8,128)(2,1)}, u32[]{:S(2)}) copy-start(bf16[2048,8,128]{0,2,1:T(8,128)(2,1)} %squeeze.6) | copy-start | bytes 12582916
  170.5 2.1 %copy-start.3 = (bf16[32,32,256]{2,1,0:T(8,128)(2,1)S(1)}, bf16[32,32,256]{2,1,0:T(8,128)(2,1)}, u32[]{:S(2)}) copy-start(bf16[32,32,256]{2,1,0:T(8,128)(2,1)} %param.9) | copy-start | bytes 1572868
  190.0 8.0 %copy-start.1 = (bf16[512,2048]{1,0:T(8,128)(2,1)S(1)}, bf16[512,2048]{1,0:T(8,128)(2,1)}, u32[]{:S(2)}) copy-start(bf16[512,2048]{1,0:T(8,128)(2,1)} %param.5) | copy-start | bytes 6291460
